TPU v7x, 32 devices: a whole 2x2x4 slice. The times are simulated.
32 devices in a mesh: row: 4 (over x, core), col: 8 (over z, y).
Axes of the slice: x: 2, y: 2, z: 4, core: 2. Of those that a mesh axis runs over, the one named last changes fastest.
Arguments:
- features: bfloat16 [8192, 256], P(('col', 'row')), may hold values from -6 to 6
- weight: bfloat16 [256, 256], replicated, may hold values from -0.375 to 0.375
- grad_out: bfloat16 [8192, 256], P(('row', 'col')), may hold values from -6 to 6
- adj_values: bfloat16 [384, 1024, 128], P('row', 'col'), may hold values from -0.15625 to 0.15625
- block_pos: int32 [4, 768], P('row', 'col'), may hold values from 0 to 127, as said below
- block_count: int32 [4, 8], P('row', 'col'), may hold values from 24 to 96, as said below
Outputs:
- activation: bfloat16 [8192, 256], P(('row', 'col'))
- grad_input: bfloat16 [8192, 256], P(('col', 'row'))
- grad_weight: float32 [256, 256], replicated
Inputs may be any that keep to these rules, and one draw needn't show every extreme that they name: `block_pos`: within one tile the block positions of all 96 slots are distinct values below 128. `block_count`: some tile has exactly 96 live slots and some tile exactly 24.
All inputs are finite; a program needn't handle non-finite values.
Results may differ from a plain program's by a relative error of at most 0.018.
Values may be sent and summed in bfloat16 or wider, within the bound.
A program may use at most 128 MiB of HBM per device.

v0:
```python
import jax
import jax.numpy as jnp
from jax import lax
from jax.sharding import PartitionSpec as P


def tile_forward(values, positions, live_count, panel, row_blocks, col_blocks):
    slots = values.shape[0]
    block_size = values.shape[1]
    width = panel.shape[1]
    groups = 6
    per_group = slots // groups
    brow = positions // col_blocks
    bcol = positions % col_blocks
    live = (jnp.arange(slots, dtype=jnp.int32) < live_count).astype(jnp.float32)
    blocks = panel.reshape(col_blocks, block_size, width)

    def step(totals, items):
        vals, rows_idx, cols_idx, alive = items
        picked = blocks[cols_idx]
        prod = jnp.einsum("kij,kjf->kif", vals, picked, preferred_element_type=jnp.float32)
        onehot = (rows_idx[None, :] == jnp.arange(row_blocks, dtype=jnp.int32)[:, None]).astype(
            jnp.float32
        ) * alive[None, :]
        return (totals + jnp.einsum("bk,kif->bif", onehot, prod), None)

    items = (
        values.reshape(groups, per_group, block_size, block_size),
        brow.reshape(groups, per_group),
        bcol.reshape(groups, per_group),
        live.reshape(groups, per_group),
    )
    start = jnp.zeros((row_blocks, block_size, width), jnp.float32)
    totals, unused = lax.scan(step, start, items)
    return totals.reshape(row_blocks * block_size, width)


def tile_backward(values, positions, live_count, grads, row_blocks, col_blocks):
    slots = values.shape[0]
    block_size = values.shape[1]
    width = grads.shape[1]
    groups = 6
    per_group = slots // groups
    brow = positions // col_blocks
    bcol = positions % col_blocks
    live = (jnp.arange(slots, dtype=jnp.int32) < live_count).astype(jnp.float32)
    blocks = grads.reshape(row_blocks, block_size, width)

    def step(totals, items):
        vals, rows_idx, cols_idx, alive = items
        picked = blocks[rows_idx]
        prod = jnp.einsum("kij,kif->kjf", vals, picked, preferred_element_type=jnp.float32)
        onehot = (cols_idx[None, :] == jnp.arange(col_blocks, dtype=jnp.int32)[:, None]).astype(
            jnp.float32
        ) * alive[None, :]
        return (totals + jnp.einsum("bk,kjf->bjf", onehot, prod), None)

    items = (
        values.reshape(groups, per_group, block_size, block_size),
        brow.reshape(groups, per_group),
        bcol.reshape(groups, per_group),
        live.reshape(groups, per_group),
    )
    start = jnp.zeros((col_blocks, block_size, width), jnp.float32)
    totals, unused = lax.scan(step, start, items)
    return totals.reshape(col_blocks * block_size, width)


def body(features, weight, grad_out, adj_values, block_pos, block_count):
    block_size = adj_values.shape[2]
    rows_tile = grad_out.shape[0] * lax.axis_size("col")
    row_blocks = rows_tile // block_size
    projected = jnp.dot(features, weight, preferred_element_type=jnp.float32).astype(jnp.bfloat16)
    panel = lax.all_gather(projected, "row", axis=0, tiled=True)
    col_blocks = panel.shape[0] // block_size
    positions = block_pos[0]
    live_count = block_count[0, 0]
    partial_value = tile_forward(adj_values, positions, live_count, panel, row_blocks, col_blocks)
    hidden = lax.psum_scatter(
        partial_value.astype(jnp.bfloat16), "col", scatter_dimension=0, tiled=True
    ).astype(jnp.float32)
    sigma = jax.nn.sigmoid(hidden)
    activation = (hidden * sigma).astype(jnp.bfloat16)
    grad_hidden = (grad_out.astype(jnp.float32) * sigma * (1.0 + hidden * (1.0 - sigma))).astype(
        jnp.bfloat16
    )
    grad_panel = lax.all_gather(grad_hidden, "col", axis=0, tiled=True)
    partial_back = tile_backward(
        adj_values, positions, live_count, grad_panel, row_blocks, col_blocks
    )
    grad_xw = lax.psum_scatter(
        partial_back.astype(jnp.bfloat16), "row", scatter_dimension=0, tiled=True
    )
    local_weight = lax.dot_general(
        features, grad_xw, (((0,), (0,)), ((), ())), preferred_element_type=jnp.float32
    )
    grad_weight = lax.psum(local_weight, ("row", "col"))
    grad_input = lax.dot_general(
        grad_xw, weight, (((1,), (1,)), ((), ())), preferred_element_type=jnp.float32
    ).astype(jnp.bfloat16)
    return (activation, grad_input, grad_weight)


def solution(mesh):
    placed = (
        P(("col", "row"), None),
        P(),
        P(("row", "col"), None),
        P("row", "col", None),
        P("row", "col"),
        P("row", "col"),
    )
    return jax.shard_map(
        body,
        mesh=mesh,
        in_specs=placed,
        out_specs=(P(("row", "col"), None), P(("col", "row"), None), P()),
        check_vma=False,
    )
```

profile of v0, /device:TPU:0, one launch (start us, length us, event | category | flops | bytes accessed | tf_op | source)
XLA Modules:
  0.0 351.3 jit_solution(11104023459522061868)
XLA Ops:
  7.7 1.3 reduce.3
  9.8 1.1 convolution_convert_fusion.1
  10.9 8.6 %all_gather.6 = bf16[1024,256]{1,0:T(8,128)(2,1)S(1)} all-gather(bf16[256,256]{1,0:T(8,128)(2,1)S(1)} %convolution_convert_fusion.1), channel_id=1, replica_groups=mesh['row'=4,'col'=8] {'row'}, dimensions={0}, use_global_device_ids=true | all-gather | bytes 655360 | tf_op jit(solution)/shard_map/all_gather | solution.py:74
  19.6 33.6 %while.22 = (s32[]{:T(128)}, f32[16,128,256]{2,0,1:T(8,128)}, s32[6,16]{1,0:T(8,128)S(1)}, bf16[6,16]{1,0:T(8,128)(2,1)S(1)}, bf16[6,16,128,128]{3,2,1,0:T(8,128...) while((s32[]{:T(128)}, f32[16,128,256]{2,0,1:T(8,128)}, ...), condition=%wide.region_1.2_spmd.clone, body=%wide.region_0.1_spmd.clone.sunk | while | flops 152045104 | bytes 9966739 | solution.py:34
  19.6 0.6 gather_fusion
  20.2 1.5 fusion.77
  21.7 2.1 select_add_fusion.2
  24.5 1.5 fusion.77
  26.0 3.7 %select_add_fusion.2 = f32[16,128,256]{2,0,1:T(8,128)} fusion(f32[16,128,256]{2,0,1:T(8,128)} %get-tuple-element.261, bf16[16,128,256]{2,1,0:T(8,128)(2,1)S(1)} %fusion.77, pred[]{:T(512)S(6)} %compare.11, bf16[16]{0:T(256)(128)(2,1)S(1)} %fusion.78, s32[16]{0:T(128)S(1)} %fusion.79), kind=kOutput, calls=%fused_computation.4.clone.1 | convolution fusion | flops 17826304 | bytes 5242977 | tf_op jit(solution)/shard_map/while/body/eval_jaxpr/bk,kif->bif/dot_general | solution.py:25
  30.4 1.5 fusion.77
  31.9 3.7 %select_add_fusion.2 = f32[16,128,256]{2,0,1:T(8,128)} fusion(f32[16,128,256]{2,0,1:T(8,128)} %get-tuple-element.261, bf16[16,128,256]{2,1,0:T(8,128)(2,1)S(1)} %fusion.77, pred[]{:T(512)S(6)} %compare.11, bf16[16]{0:T(256)(128)(2,1)S(1)} %fusion.78, s32[16]{0:T(128)S(1)} %fusion.79), kind=kOutput, calls=%fused_computation.4.clone.1 | convolution fusion | flops 17826304 | bytes 5242977 | tf_op jit(solution)/shard_map/while/body/eval_jaxpr/bk,kif->bif/dot_general | solution.py:25
  35.6 0.6 gather_fusion
  36.2 1.5 fusion.77
  37.7 3.7 %select_add_fusion.2 = f32[16,128,256]{2,0,1:T(8,128)} fusion(f32[16,128,256]{2,0,1:T(8,128)} %get-tuple-element.261, bf16[16,128,256]{2,1,0:T(8,128)(2,1)S(1)} %fusion.77, pred[]{:T(512)S(6)} %compare.11, bf16[16]{0:T(256)(128)(2,1)S(1)} %fusion.78, s32[16]{0:T(128)S(1)} %fusion.79), kind=kOutput, calls=%fused_computation.4.clone.1 | convolution fusion | flops 17826304 | bytes 5242977 | tf_op jit(solution)/shard_map/while/body/eval_jaxpr/bk,kif->bif/dot_general | solution.py:25
  42.1 1.5 fusion.77
  43.6 3.7 %select_add_fusion.2 = f32[16,128,256]{2,0,1:T(8,128)} fusion(f32[16,128,256]{2,0,1:T(8,128)} %get-tuple-element.261, bf16[16,128,256]{2,1,0:T(8,128)(2,1)S(1)} %fusion.77, pred[]{:T(512)S(6)} %compare.11, bf16[16]{0:T(256)(128)(2,1)S(1)} %fusion.78, s32[16]{0:T(128)S(1)} %fusion.79), kind=kOutput, calls=%fused_computation.4.clone.1 | convolution fusion | flops 17826304 | bytes 5242977 | tf_op jit(solution)/shard_map/while/body/eval_jaxpr/bk,kif->bif/dot_general | solution.py:25
  48.0 1.5 fusion.77
  49.5 3.7 %select_add_fusion.2 = f32[16,128,256]{2,0,1:T(8,128)} fusion(f32[16,128,256]{2,0,1:T(8,128)} %get-tuple-element.261, bf16[16,128,256]{2,1,0:T(8,128)(2,1)S(1)} %fusion.77, pred[]{:T(512)S(6)} %compare.11, bf16[16]{0:T(256)(128)(2,1)S(1)} %fusion.78, s32[16]{0:T(128)S(1)} %fusion.79), kind=kOutput, calls=%fused_computation.4.clone.1 | convolution fusion | flops 17826304 | bytes 5242977 | tf_op jit(solution)/shard_map/while/body/eval_jaxpr/bk,kif->bif/dot_general | solution.py:25
  53.2 1.7 convert_element_type.39
  55.0 1.3 copy.11
  56.4 65.1 %reduce-scatter.3.cloned.1.call-done = bf16[256,256]{1,0:T(8,128)(2,1)} async-done(((bf16[2048,256]{1,0:T(8,128)(2,1)}), bf16[256,256]{1,0:T(8,128)(2,1)}) %reduce-scatter.3.cloned.1.call-update) | async-done | bytes 131088 | tf_op jit(solution)/shard_map/reduce_scatter | solution.py:79
  121.5 1.7 fusion.43
  123.3 40.2 %all-gather.2.cloned.1.call-done = bf16[2048,256]{1,0:T(8,128)(2,1)} async-done(((bf16[256,256]{1,0:T(8,128)(2,1)}), bf16[2048,256]{1,0:T(8,128)(2,1)}) %all-gather.2.cloned.1.call-update) | async-done | bytes 1048592 | tf_op jit(solution)/shard_map/all_gather | solution.py:87
  163.5 25.3 %while.23 = (s32[]{:T(128)}, f32[8,128,256]{2,0,1:T(8,128)S(1)}, s32[6,16]{1,0:T(8,128)S(1)}, bf16[6,16]{1,0:T(8,128)(2,1)S(1)}, bf16[6,16,128,128]{3,2,1,0:T(8,...) while((s32[]{:T(128)}, f32[8,128,256]{2,0,1:T(8,128)S(1)}, ...), condition=%wide.region_4.5_spmd.clone, body=%wide.region_3.4_spmd.clone.sunk | while | flops 143131952 | bytes 7869587 | solution.py:65
  163.5 1.8 gather_fusion.1
  165.4 1.5 fusion.85
  166.9 0.8 fusion.88
  167.7 1.8 gather_fusion.1
  169.6 1.5 fusion.85
  171.2 0.8 fusion.88
  172.0 1.8 gather_fusion.1
  173.8 1.5 fusion.85
  175.4 0.8 fusion.88
  176.2 1.8 gather_fusion.1
  178.0 1.5 fusion.85
  179.6 0.8 fusion.88
  180.4 1.8 gather_fusion.1
  182.3 1.5 fusion.85
  183.8 0.8 fusion.88
  184.7 1.8 gather_fusion.1
  186.5 1.5 fusion.85
  188.1 0.8 fusion.88
  188.9 1.1 copy.25
  190.0 20.4 %reduce-scatter.5.cloned.1.call-done = bf16[256,256]{1,0:T(8,128)(2,1)} async-done(((bf16[1024,256]{1,0:T(8,128)(2,1)}), bf16[256,256]{1,0:T(8,128)(2,1)}) %reduce-scatter.5.cloned.1.call-update) | async-done | bytes 131088 | tf_op jit(solution)/shard_map/reduce_scatter | solution.py:91
  210.5 1.8 convolution_bitcast_fusion
  212.3 1.8 convolution_convert_fusion
  214.1 128.9 %all-reduce.2.cloned.1.call-done = f32[256,256]{0,1:T(8,128)} async-done(((f32[256,256]{0,1:T(8,128)}), f32[256,256]{0,1:T(8,128)}) %all-reduce.2.cloned.1.call-update) | async-done | bytes 262160 | tf_op jit(solution)/shard_map/psum | solution.py:97
  343.0 1.8 copy.13
  (72 shorter events, 3.8 us)
Async XLA Ops:
  7.2 2.7 copy-start
  7.2 114.3 %reduce-scatter.3.cloned.1.call-start = ((), (), s32[]{:S(2)}) async-start(), calls=%async_computation.2 | async-start | bytes 1179648 | tf_op jit(solution)/shard_map/reduce_scatter | solution.py:79
  54.9 66.5 %copy-start.2 = (bf16[256,256]{1,0:T(8,128)(2,1)S(1)}, bf16[256,256]{1,0:T(8,128)(2,1)}, u32[]{:S(2)}) copy-start(bf16[256,256]{1,0:T(8,128)(2,1)} %param.12) | copy-start | bytes 393220
  56.3 107.2 %all-gather.2.cloned.1.call-start = ((), (), s32[]{:S(2)}) async-start(), calls=%async_computation.3 | async-start | bytes 1179648 | tf_op jit(solution)/shard_map/all_gather | solution.py:87
  123.2 87.3 %reduce-scatter.5.cloned.1.call-start = ((), (), s32[]{:S(2)}) async-start(), calls=%async_computation.4 | async-start | bytes 655360 | tf_op jit(solution)/shard_map/reduce_scatter | solution.py:91
  188.8 23.5 %copy-start.1 = (bf16[256,256]{1,0:T(8,128)(2,1)S(1)}, bf16[256,256]{1,0:T(8,128)(2,1)}, u32[]{:S(2)}) copy-start(bf16[256,256]{1,0:T(8,128)(2,1)} %param.11) | copy-start | bytes 393220
  190.0 153.0 %all-reduce.2.cloned.1.call-start = ((), (), s32[]{:S(2)}) async-start(), calls=%async_computation.5 | async-start | bytes 524288 | tf_op jit(solution)/shard_map/psum | solution.py:97
Sparse Core Ops, SparseCore 0:
  56.4 64.9 reduce-scatter.2
  124.2 39.3 all-gather.1
  190.1 20.3 reduce-scatter.4
  216.4 126.5 all-reduce.1
where the time goes:
time: 353 us; the launch traced here: 351 us
  waiting for transfers between devices  255 us (72%)
  matrix products  47.9 us (14%)
  local copies, waits for them, and re-layouts  19.8 us (6%)
  between operations  14.5 us (4%)
  blocking collectives  8.65 us (2%)
  other arithmetic  4.97 us (1%)
    psum x1, waiting for transfers between devices, body(): grad_weight = lax.psum(local_weight, ('row', 'col'))  129 us
    reduce_scatter x1, waiting for transfers between devices, body(): lax.psum_scatter(partial_value.astype(jnp.bfloat16), 'col', scatter_dimen...  65.1 us
    all_gather x1, waiting for transfers between devices, body(): grad_panel = lax.all_gather(grad_hidden, 'col', axis=0, tiled=True)  40.2 us
    dot_general x6, matrix products, step(): return (totals + jnp.einsum('bk,kif->bif', onehot, prod), None)  20.7 us
    reduce_scatter x1, waiting for transfers between devices, body(): lax.psum_scatter(partial_back.astype(jnp.bfloat16), 'row', scatter_dimens...  20.4 us
    gather x6, local copies, waits for them, and re-layouts, step(): picked = blocks[rows_idx]  11 us
    dot_general x6, matrix products, step(): jnp.einsum('kij,kif->kjf', vals, picked, preferred_element_type=jnp.float32)  9.18 us
    dot_general x6, matrix products, step(): jnp.einsum('kij,kjf->kif', vals, picked, preferred_element_type=jnp.float32)  8.8 us
  transfers between devices with their start and end apart: 4, of which 4 were waited for; matrix products, arithmetic and copies ran while one was open for 1% of the time, Pallas kernels for 0%

commit v1 on v0

--- a/solution.py
+++ b/solution.py
@@ -1,7 +1,16 @@
+import functools
 import jax
 import jax.numpy as jnp
 from jax import lax
 from jax.sharding import PartitionSpec as P
+
+
+def test_lots_all(shard_in, axis_id):
+    carry = jnp.sum(lax.all_gather(shard_in, axis_name=axis_id), axis=0)
+    return carry
+
+
+shape_sides = functools.partial(test_lots_all, axis_id=("row", "col"))
 
 
 def tile_forward(values, positions, live_count, panel, row_blocks, col_blocks):
@@ -94,7 +103,7 @@
     local_weight = lax.dot_general(
         features, grad_xw, (((0,), (0,)), ((), ())), preferred_element_type=jnp.float32
     )
-    grad_weight = lax.psum(local_weight, ("row", "col"))
+    grad_weight = shape_sides(local_weight)
     grad_input = lax.dot_general(
         grad_xw, weight, (((1,), (1,)), ((), ())), preferred_element_type=jnp.float32
     ).astype(jnp.bfloat16)

time: 353 us -> 305 us (0.86)
  waiting for transfers between devices: 255 us -> 205 us
  local copies, waits for them, and re-layouts: 19.8 us -> 36.5 us
  matrix products: 47.9 us -> 32.2 us
    psum x1 -> x0, waiting for transfers between devices: 129 us -> none  [body(): grad_weight = lax.psum(local_weight, ('row', 'col'))]
    all_gather x0 -> x1, waiting for transfers between devices: none -> 83.7 us  [test_lots_all(): carry = jnp.sum(lax.all_gather(shard_in, axis_name=axis_id), axis=0)]
    dot_general x6, matrix products: 20.7 us -> 5.35 us  [step(): return (totals + jnp.einsum('bk,kif->bif', onehot, prod), None)]
    unnamed x8 -> x10, local copies, waits for them, and re-layouts: 2.32 us -> 12.8 us
    gather x6, local copies, waits for them, and re-layouts: 3.68 us -> 9.93 us  [step(): picked = blocks[cols_idx]]
    all_gather x1, waiting for transfers between devices: 40.2 us -> 35.6 us  [body(): grad_panel = lax.all_gather(grad_hidden, 'col', axis=0, tiled=True)]
  transfers between devices with their start and end apart: 4 -> 4, of which waited for: 4 -> 4; matrix products, arithmetic and copies ran while one was open for 1% -> 2% of each run, Pallas kernels for 0% -> 0%
where the time goes in v1:
time: 305 us; the launch traced here: 304 us
  waiting for transfers between devices  205 us (67%)
  local copies, waits for them, and re-layouts  36.5 us (12%)
  matrix products  32.2 us (11%)
  between operations  14.5 us (5%)
  blocking collectives  9.1 us (3%)
  other arithmetic  5.3 us (2%)
    all_gather x1, waiting for transfers between devices, test_lots_all(): carry = jnp.sum(lax.all_gather(shard_in, axis_name=axis_id), axis=0)  83.7 us
    reduce_scatter x1, waiting for transfers between devices, body(): lax.psum_scatter(partial_value.astype(jnp.bfloat16), 'col', scatter_dimen...  65.2 us
    all_gather x1, waiting for transfers between devices, body(): grad_panel = lax.all_gather(grad_hidden, 'col', axis=0, tiled=True)  35.6 us
    reduce_scatter x1, waiting for transfers between devices, body(): lax.psum_scatter(partial_back.astype(jnp.bfloat16), 'row', scatter_dimens...  20.4 us
    unnamed x10, local copies, waits for them, and re-layouts  12.8 us
    gather x6, local copies, waits for them, and re-layouts, step(): picked = blocks[rows_idx]  11 us
    gather x6, local copies, waits for them, and re-layouts, step(): picked = blocks[cols_idx]  9.93 us
    all_gather x1, blocking collectives, body(): panel = lax.all_gather(projected, 'row', axis=0, tiled=True)  9.1 us
  transfers between devices with their start and end apart: 4, of which 4 were waited for; matrix products, arithmetic and copies ran while one was open for 2% of the time, Pallas kernels for 0%

profile of v1, /device:TPU:0, one launch (start us, length us, event | category | flops | bytes accessed | tf_op | source)
XLA Modules:
  0.0 303.6 jit_solution(11827327652055357949)
XLA Ops:
  8.4 1.3 reduce.3
  9.9 1.1 convolution_convert_fusion.1
  11.0 9.1 %all_gather.12 = bf16[1024,256]{1,0:T(8,128)(2,1)} all-gather(bf16[256,256]{1,0:T(8,128)(2,1)S(1)} %convolution_convert_fusion.1), channel_id=1, replica_groups=mesh['row'=4,'col'=8] {'row'}, dimensions={0}, use_global_device_ids=true | all-gather | bytes 655360 | tf_op jit(solution)/shard_map/all_gather | solution.py:83
  20.1 24.7 %while.22 = (s32[]{:T(128)}, f32[16,128,256]{2,0,1:T(8,128)S(1)}, s32[6,16]{1,0:T(8,128)S(1)}, bf16[6,16]{1,0:T(8,128)(2,1)S(1)}, bf16[6,16,128,128]{3,2,1,0:T(8...) while((s32[]{:T(128)}, f32[16,128,256]{2,0,1:T(8,128)S(1)}, ...), condition=%wide.region_1.2_spmd.clone, body=%wide.region_0.1_spmd.clone.sunk | while | flops 152045104 | bytes 9966239 | solution.py:43
  20.1 1.7 gather_fusion
  21.8 1.5 fusion.77
  23.2 0.9 select_add_fusion.2
  24.2 1.7 gather_fusion
  25.9 1.5 fusion.77
  27.3 0.9 select_add_fusion.2
  28.3 1.7 gather_fusion
  30.0 1.5 fusion.77
  31.5 0.9 select_add_fusion.2
  32.4 1.7 gather_fusion
  34.1 1.5 fusion.77
  35.6 0.9 select_add_fusion.2
  36.6 1.7 gather_fusion
  38.2 1.5 fusion.77
  39.7 0.9 select_add_fusion.2
  40.7 1.7 gather_fusion
  42.3 1.5 fusion.77
  43.8 0.9 select_add_fusion.2
  44.9 1.3 copy.16
  46.3 65.2 %reduce-scatter.3.cloned.1.call-done = bf16[256,256]{1,0:T(8,128)(2,1)} async-done(((bf16[2048,256]{1,0:T(8,128)(2,1)}), bf16[256,256]{1,0:T(8,128)(2,1)}) %reduce-scatter.3.cloned.1.call-update) | async-done | bytes 131088 | tf_op jit(solution)/shard_map/reduce_scatter | solution.py:88
  111.5 1.7 fusion.43
  113.3 4.6 %copy.14 = bf16[96,128,128]{1,2,0:T(8,128)(2,1)} copy(bf16[96,128,128]{2,1,0:T(8,128)(2,1)} %bitcast.90) | data formatting | bytes 6291456 | tf_op args[3]
  117.9 35.6 %all-gather.4.cloned.1.call-done = bf16[2048,256]{1,0:T(8,128)(2,1)} async-done(((bf16[256,256]{1,0:T(8,128)(2,1)}), bf16[2048,256]{1,0:T(8,128)(2,1)}) %all-gather.4.cloned.1.call-update) | async-done | bytes 1048592 | tf_op jit(solution)/shard_map/all_gather | solution.py:96
  153.5 24.9 %while.23 = (s32[]{:T(128)}, f32[8,128,256]{2,0,1:T(8,128)S(1)}, s32[6,16]{1,0:T(8,128)S(1)}, bf16[6,16]{1,0:T(8,128)(2,1)S(1)}, bf16[6,16,128,128]{2,3,1,0:T(8,...) while((s32[]{:T(128)}, f32[8,128,256]{2,0,1:T(8,128)S(1)}, ...), condition=%wide.region_4.5_spmd.clone, body=%wide.region_3.4_spmd.clone.sunk | while | flops 143131952 | bytes 7869087 | solution.py:74
  153.5 1.8 gather_fusion.1
  155.4 1.5 fusion.85
  157.7 1.8 gather_fusion.1
  159.5 1.5 fusion.85
  161.9 1.8 gather_fusion.1
  163.7 1.5 fusion.85
  166.0 1.8 gather_fusion.1
  167.9 1.5 fusion.85
  170.2 1.8 gather_fusion.1
  172.0 1.5 fusion.85
  174.3 1.8 gather_fusion.1
  176.2 1.5 fusion.85
  178.4 1.1 copy.30
  179.6 20.4 %reduce-scatter.5.cloned.1.call-done = bf16[256,256]{1,0:T(8,128)(2,1)} async-done(((bf16[1024,256]{1,0:T(8,128)(2,1)}), bf16[256,256]{1,0:T(8,128)(2,1)}) %reduce-scatter.5.cloned.1.call-update) | async-done | bytes 131088 | tf_op jit(solution)/shard_map/reduce_scatter | solution.py:100
  200.0 1.8 convolution_bitcast_fusion
  201.9 1.8 convolution_convert_fusion
  203.7 83.7 %all-gather.6.cloned.1.call-done = f32[8192,256]{0,1:T(8,128)} async-done(((f32[256,256]{0,1:T(8,128)}), f32[8192,256]{0,1:T(8,128)}) %all-gather.6.cloned.1.call-update) | async-done | bytes 8388624 | tf_op jit(solution)/shard_map/all_gather | solution.py:9
  287.4 6.8 %copy.20 = f32[32,8,32,256]{3,2,1,0:T(8,128)S(1)} copy(f32[32,8,32,256]{3,1,2,0:T(8,128)} %bitcast.92) | data formatting | bytes 16777216
  294.3 1.9 bitcast_reduce_fusion
  296.2 0.8 copy.18
  (75 shorter events, 6.0 us)
Async XLA Ops:
  7.2 2.7 copy-start
  7.2 104.3 %reduce-scatter.3.cloned.1.call-start = ((), (), s32[]{:S(2)}) async-start(), calls=%async_computation.2 | async-start | bytes 1179648 | tf_op jit(solution)/shard_map/reduce_scatter | solution.py:88
  44.9 66.6 %copy-start.2 = (bf16[256,256]{1,0:T(8,128)(2,1)S(1)}, bf16[256,256]{1,0:T(8,128)(2,1)}, u32[]{:S(2)}) copy-start(bf16[256,256]{1,0:T(8,128)(2,1)} %param.12) | copy-start | bytes 393220
  46.2 107.3 %all-gather.4.cloned.1.call-start = ((), (), s32[]{:S(2)}) async-start(), calls=%async_computation.3 | async-start | bytes 1179648 | tf_op jit(solution)/shard_map/all_gather | solution.py:96
  113.2 86.8 %reduce-scatter.5.cloned.1.call-start = ((), (), s32[]{:S(2)}) async-start(), calls=%async_computation.4 | async-start | bytes 655360 | tf_op jit(solution)/shard_map/reduce_scatter | solution.py:100
  178.4 23.5 %copy-start.1 = (bf16[256,256]{1,0:T(8,128)(2,1)S(1)}, bf16[256,256]{1,0:T(8,128)(2,1)}, u32[]{:S(2)}) copy-start(bf16[256,256]{1,0:T(8,128)(2,1)} %param.11) | copy-start | bytes 393220
  179.6 107.9 %all-gather.6.cloned.1.call-start = ((), (), s32[]{:S(2)}) async-start(), calls=%async_computation.5 | async-start | bytes 8650752 | tf_op jit(solution)/shard_map/all_gather | solution.py:9
Sparse Core Ops, SparseCore 0:
  46.3 65.0 reduce-scatter.2
  114.2 39.2 all-gather.3
  179.7 20.3 reduce-scatter.4
  203.4 84.0 all-gather.5
